TPU v7x, 256 devices: a whole 4x4x8 slice. The times are simulated.
256 devices in a mesh: segment: 4 (over z_lo, core), zero: 64 (over x, y, z_hi).
Axes of the slice: x: 4, y: 4, z: 8 (z_hi: 4, z_lo: 2; z = z_hi * 2 + z_lo), core: 2. Of those that a mesh axis runs over, the one named last changes fastest.
Arguments:
- inputs: bfloat16 [2, 2, 8192, 2048], P(None, None, 'zero'), may hold values from -6 to 6
- cotangent: bfloat16 [2, 2, 8192, 2048], P(None, None, 'zero'), may hold values from -0.078125 to 0.078125
- norm_gain: bfloat16 [4, 2048], P('segment', 'zero'), may hold values from 0.099609375 to 1.8984375
- proj_in: bfloat16 [4, 2048, 256], P('segment', 'zero'), may hold values from -0.125 to 0.125
- proj_out: bfloat16 [4, 256, 2048], P('segment', 'zero'), may hold values from -0.375 to 0.375
Outputs:
- grad_norm_gain: float32 [4, 2048], P('segment', 'zero')
- grad_proj_in: float32 [4, 2048, 256], P('segment', 'zero')
- grad_proj_out: float32 [4, 256, 2048], P('segment', 'zero')
All inputs are finite; a program needn't handle non-finite values.
Results may differ from a plain program's by a relative error of at most 0.012.
Values may be sent and summed in bfloat16 or wider, within the bound.
No kernel may reach another device: no remote copies, remote signals or barrier semaphores. Data moves between devices by JAX's collectives and lax.ppermute only.
A program may use at most 64 MiB of HBM per device.

v0:
```python
import jax
import jax.numpy as jnp
from jax import lax
from jax.sharding import PartitionSpec as P

gelu_coeff = 0.7978845608028654
cubic_coeff = 0.044715
norm_eps = 1e-05


def partner(value, axis, stride):
    return lax.ppermute(value, axis, [(i, i ^ 1 << stride) for i in range(lax.axis_size(axis))])


def from_behind(block, axis, distance):
    devices = range(lax.axis_size(axis))
    route = [(i - distance, i) for i in devices if i - distance in devices]
    return lax.ppermute(block, axis, route)


def gelu_tanh(values):
    return (
        0.5
        * values
        * (1.0 + jnp.tanh(gelu_coeff * (values + cubic_coeff * values * values * values)))
    )


def gelu_slope(values):
    inner = jnp.tanh(gelu_coeff * (values + cubic_coeff * values * values * values))
    return 0.5 * (1.0 + inner) + 0.5 * values * (1.0 - inner * inner) * gelu_coeff * (
        1.0 + 3.0 * cubic_coeff * values * values
    )


def contract(left, right, left_dim, right_dim):
    return lax.dot_general(
        left, right, (((left_dim,), (right_dim,)), ((), ())), preferred_element_type=jnp.float32
    )


def layer_forward(state, gain, weight_in, weight_out):
    as_float = state.astype(jnp.float32)
    centered = as_float - jnp.mean(as_float, axis=-1, keepdims=True)
    variance = jnp.mean(centered * centered, axis=-1, keepdims=True)
    recip_std = lax.rsqrt(variance + norm_eps)
    hatted = centered * recip_std
    normed = (hatted * gain.astype(jnp.float32)).astype(jnp.bfloat16)
    preact = jnp.dot(normed, weight_in, preferred_element_type=jnp.float32)
    gelu_out = gelu_tanh(preact).astype(jnp.bfloat16)
    result = (as_float + jnp.dot(gelu_out, weight_out, preferred_element_type=jnp.float32)).astype(
        jnp.bfloat16
    )
    return (result, (hatted, recip_std, normed, preact, gelu_out))


def layer_backward(state, upstream, gain, weight_in, weight_out):
    result, saved = layer_forward(state, gain, weight_in, weight_out)
    hatted, recip_std, normed, preact, gelu_out = saved
    grad_out = contract(gelu_out, upstream, 0, 0)
    grad_act = contract(upstream, weight_out, 1, 1)
    grad_pre = (grad_act * gelu_slope(preact)).astype(jnp.bfloat16)
    grad_in = contract(normed, grad_pre, 0, 0)
    grad_normed = contract(grad_pre, weight_in, 1, 1)
    grad_gain = jnp.sum(grad_normed * hatted, axis=0)
    grad_hat = grad_normed * gain.astype(jnp.float32)
    through = recip_std * (
        grad_hat
        - jnp.mean(grad_hat, axis=-1, keepdims=True)
        - hatted * jnp.mean(grad_hat * hatted, axis=-1, keepdims=True)
    )
    grad_state = (upstream.astype(jnp.float32) + through).astype(jnp.bfloat16)
    return (grad_state, grad_in, grad_out, grad_gain)


def pick_slot(stack, index):
    return lax.dynamic_index_in_dim(stack, index, 0, keepdims=False)


def keep_slot(stack, index, valid, value):
    merged = jnp.where(valid, value, pick_slot(stack, index))
    return lax.dynamic_update_index_in_dim(stack, merged, index, 0)


def per_device(inputs, cotangent, norm_gain, proj_in, proj_out):
    segment_count = lax.axis_size("segment")
    segment_idx = lax.axis_index("segment")
    bit_count = segment_count.bit_length() - 1
    mirror_in, mirror_out, mirror_gain = (proj_in, proj_out, norm_gain)
    for bit_pos in range(bit_count):
        mirror_in, mirror_out, mirror_gain = partner(
            (mirror_in, mirror_out, mirror_gain), "segment", bit_pos
        )
    gathered = (
        lax.all_gather(proj_in, "zero", axis=1, tiled=True),
        lax.all_gather(mirror_in, "zero", axis=1, tiled=True),
        lax.all_gather(proj_out, "zero", axis=1, tiled=True),
        lax.all_gather(mirror_out, "zero", axis=1, tiled=True),
        lax.all_gather(norm_gain, "zero", axis=1, tiled=True),
        lax.all_gather(mirror_gain, "zero", axis=1, tiled=True),
    )
    down_in, upper_in = (gathered[0][0], gathered[1][0])
    down_out, upper_out = (gathered[2][0], gathered[3][0])
    down_gain, upper_gain = (gathered[4][0], gathered[5][0])
    micro_count = inputs.shape[1]
    rows = inputs.shape[2]
    width = inputs.shape[3]
    tick_total = micro_count + segment_count - 1
    is_first = segment_idx == 0
    is_last = segment_idx == segment_count - 1
    last_slot = micro_count - 1
    stash_down = jnp.zeros((micro_count, rows, width), jnp.bfloat16)
    stash_upper = jnp.zeros((micro_count, rows, width), jnp.bfloat16)
    recv_down = jnp.zeros((rows, width), jnp.bfloat16)
    recv_upper = jnp.zeros((rows, width), jnp.bfloat16)
    for tick_num in range(tick_total):
        micro_down = tick_num - segment_idx
        micro_upper = tick_num - (segment_count - 1 - segment_idx)
        valid_down = (micro_down >= 0) & (micro_down < micro_count)
        valid_upper = (micro_upper >= 0) & (micro_upper < micro_count)
        slot_down = jnp.clip(micro_down, 0, last_slot)
        slot_upper = jnp.clip(micro_upper, 0, last_slot)
        enter_down = jnp.where(is_first, pick_slot(inputs[0], slot_down), recv_down)
        enter_upper = jnp.where(is_last, pick_slot(inputs[1], slot_upper), recv_upper)
        stash_down = keep_slot(stash_down, slot_down, valid_down, enter_down)
        stash_upper = keep_slot(stash_upper, slot_upper, valid_upper, enter_upper)
        leave_down, unused_down = layer_forward(enter_down, down_gain, down_in, down_out)
        leave_upper, unused_upper = layer_forward(enter_upper, upper_gain, upper_in, upper_out)
        if tick_num + 1 < tick_total:
            recv_down = from_behind(leave_down, "segment", 1)
            recv_upper = from_behind(leave_upper, "segment", -1)
    acc_down_in = jnp.zeros(down_in.shape, jnp.float32)
    acc_down_out = jnp.zeros(down_out.shape, jnp.float32)
    acc_down_gain = jnp.zeros(down_gain.shape, jnp.float32)
    acc_upper_in = jnp.zeros(upper_in.shape, jnp.float32)
    acc_upper_out = jnp.zeros(upper_out.shape, jnp.float32)
    acc_upper_gain = jnp.zeros(upper_gain.shape, jnp.float32)
    back_recv_down = jnp.zeros((rows, width), jnp.bfloat16)
    back_recv_upper = jnp.zeros((rows, width), jnp.bfloat16)
    for tick_num in range(tick_total):
        micro_down = tick_num - (segment_count - 1 - segment_idx)
        micro_upper = tick_num - segment_idx
        valid_down = (micro_down >= 0) & (micro_down < micro_count)
        valid_upper = (micro_upper >= 0) & (micro_upper < micro_count)
        slot_down = jnp.clip(micro_down, 0, last_slot)
        slot_upper = jnp.clip(micro_upper, 0, last_slot)
        upstream_down = jnp.where(is_last, pick_slot(cotangent[0], slot_down), back_recv_down)
        upstream_upper = jnp.where(is_first, pick_slot(cotangent[1], slot_upper), back_recv_upper)
        back_down, grad_in, grad_out, grad_gain = layer_backward(
            pick_slot(stash_down, slot_down), upstream_down, down_gain, down_in, down_out
        )
        acc_down_in = acc_down_in + jnp.where(valid_down, grad_in, 0.0)
        acc_down_out = acc_down_out + jnp.where(valid_down, grad_out, 0.0)
        acc_down_gain = acc_down_gain + jnp.where(valid_down, grad_gain, 0.0)
        back_upper, grad_in, grad_out, grad_gain = layer_backward(
            pick_slot(stash_upper, slot_upper), upstream_upper, upper_gain, upper_in, upper_out
        )
        acc_upper_in = acc_upper_in + jnp.where(valid_upper, grad_in, 0.0)
        acc_upper_out = acc_upper_out + jnp.where(valid_upper, grad_out, 0.0)
        acc_upper_gain = acc_upper_gain + jnp.where(valid_upper, grad_gain, 0.0)
        if tick_num + 1 < tick_total:
            back_recv_down = from_behind(back_down, "segment", -1)
            back_recv_upper = from_behind(back_upper, "segment", 1)
    passed_in, passed_out, passed_gain = (acc_upper_in, acc_upper_out, acc_upper_gain)
    for bit_pos in range(bit_count):
        passed_in, passed_out, passed_gain = (
            partner(passed_in.astype(jnp.bfloat16), "segment", bit_pos).astype(passed_in.dtype),
            partner(passed_out.astype(jnp.bfloat16), "segment", bit_pos).astype(passed_out.dtype),
            partner(passed_gain.astype(jnp.bfloat16), "segment", bit_pos).astype(passed_gain.dtype),
        )
    total_in, total_out, total_gain = (
        lax.psum_scatter(acc_down_in + passed_in, "zero", scatter_dimension=0, tiled=True),
        lax.psum_scatter(acc_down_out + passed_out, "zero", scatter_dimension=0, tiled=True),
        lax.psum_scatter(acc_down_gain + passed_gain, "zero", scatter_dimension=0, tiled=True),
    )
    return (total_gain[None], total_in[None], total_out[None])


def solution(mesh):
    return jax.shard_map(
        per_device,
        mesh=mesh,
        in_specs=(
            P(None, None, "zero", None),
            P(None, None, "zero", None),
            P("segment", "zero"),
            P("segment", "zero", None),
            P("segment", "zero", None),
        ),
        out_specs=(P("segment", "zero"), P("segment", "zero", None), P("segment", "zero", None)),
        check_vma=False,
    )
```

profile of v0, /device:TPU:32, one launch (start us, length us, event | category | flops | bytes accessed | tf_op | source)
XLA Modules:
  0.0 1634.1 jit_solution(740983835067146527)
XLA Ops:
  32.5 199.0 %all-reduce.4 = (bf16[2048]{0:T(1024)(128)(2,1)S(1)}, bf16[2048]{0:T(1024)(128)(2,1)S(1)}) all-reduce(bf16[2048]{0:T(1024)(128)(2,1)S(1)} %dynamic-update-slice.1, bf16[2048]{0:T(1024)(128)(2,1)S(1)} %dynamic-update-slice), channel_id=1, replica_groups=mesh['segment'=4,'zero'=64] {'zero'}, use_global_device_ids=true, to_apply=%add.1 | all-reduce | flops 4096 | bytes 16384
  231.6 3.2 copy.12
  234.8 3.5 fusion.18
  241.1 8.1 all-gather.9.cloned.1.call-done
  249.2 3.2 copy.13
  252.4 75.1 %all-gather.11.cloned.1.call-done = bf16[1,2048,256]{2,1,0:T(8,128)(2,1)} async-done(((bf16[1,32,256]{2,1,0:T(8,128)(2,1)}), bf16[1,2048,256]{2,1,0:T(8,128)(2,1)}) %all-gather.11.cloned.1.call-update) | async-done | bytes 1048592 | tf_op jit(solution)/shard_map/all_gather | solution.py:96
  327.5 3.2 fusion.22
  335.2 3.5 fusion.19
  338.6 3.2 collective-permute-start.1
  346.3 3.5 fusion.23
  349.8 2.8 collective-permute-start.15
  357.2 3.5 fusion.20
  360.7 2.6 collective-permute-start.2
  367.9 3.5 fusion.24
  371.3 3.1 collective-permute-start.16
  379.0 3.5 fusion.21
  389.1 3.5 fusion.25
  392.6 3.5 collective-permute-start.17
  413.1 2.3 collective-permute-start.18
  419.8 3.3 collective-permute-start.5
  425.9 2.3 collective-permute-start.19
  432.1 3.8 collective-permute-start.6
  443.1 6.1 collective-permute-done.20
  455.1 6.9 collective-permute-done.21
  468.8 8.8 collective-permute-done.7
  478.4 16.5 %collective-permute-done.27 = bf16[256,2048]{1,0:T(8,128)(2,1)S(1)} collective-permute-done((bf16[256,2048]{1,0:T(8,128)(2,1)S(1)}, bf16[256,2048]{1,0:T(8,128)(2,1)S(1)}, u32[]{:S(2)}, u32[]{:S(2)}) %collective-permute-start.27) | collective-permute-done | bytes 1048608 | tf_op jit(solution)/shard_map/ppermute | solution.py:12
  498.9 2.6 collective-permute-start.25
  505.6 17.5 %collective-permute-done.25 = bf16[2048,256]{1,0:T(8,128)(2,1)S(1)} collective-permute-done((bf16[2048,256]{1,0:T(8,128)(2,1)}, bf16[2048,256]{1,0:T(8,128)(2,1)S(1)}, u32[]{:S(2)}, u32[]{:S(2)}) %collective-permute-start.25) | collective-permute-done | bytes 1048608 | tf_op jit(solution)/shard_map/ppermute | solution.py:12
  529.9 2.7 collective-permute-done.23
  532.7 194.3 %all-reduce.2 = f32[2048]{0:T(1024)S(1)} all-reduce(f32[2048]{0:T(1024)S(1)} %convert_add_fusion.2), channel_id=2, replica_groups=mesh['segment'=4,'zero'=64] {'zero'}, use_global_device_ids=true, to_apply=%region_62.63.clone | all-reduce | flops 2048 | bytes 16384
  727.7 509.5 %all-reduce.7.cloned.1.call-done = f32[256,2048]{1,0:T(8,128)} async-done(((f32[256,2048]{1,0:T(8,128)}), f32[256,2048]{1,0:T(8,128)}) %all-reduce.7.cloned.1.call-update) | async-done | bytes 2097168
  1238.6 388.4 %reduce-scatter.2.cloned.1.call-done = f32[32,256]{1,0:T(8,128)} async-done(((f32[2048,256]{1,0:T(8,128)}), f32[32,256]{1,0:T(8,128)}) %reduce-scatter.2.cloned.1.call-update) | async-done | bytes 32784 | tf_op jit(solution)/shard_map/reduce_scatter | solution.py:172
  (337 shorter events, 119.9 us)
Async XLA Ops:
  7.2 224.5 %all-gather.5.cloned.1.call-start = ((), (), s32[]{:S(2)}) async-start(), calls=%async_computation.1 | async-start | bytes 2129920 | tf_op jit(solution)/shard_map/all_gather | solution.py:97
  8.6 226.2 %all-gather.7.cloned.1.call-start = ((), (), s32[]{:S(2)}) async-start(), calls=%async_computation.2 | async-start | bytes 1064960 | tf_op jit(solution)/shard_map/all_gather | solution.py:95
  9.3 239.9 %all-gather.9.cloned.1.call-start = ((), (), s32[]{:S(2)}) async-start(), calls=%async_computation.3 | async-start | bytes 2129920 | tf_op jit(solution)/shard_map/all_gather | solution.py:98
  10.9 3.9 collective-permute-start.9
  15.5 312.0 %all-gather.11.cloned.1.call-start = ((), (), s32[]{:S(2)}) async-start(), calls=%async_computation.4 | async-start | bytes 1064960 | tf_op jit(solution)/shard_map/all_gather | solution.py:96
  15.5 3.0 collective-permute-start.12
  15.6 13.2 collective-permute-start.10
  18.5 3.8 collective-permute-start.13
  23.0 1214.2 %all-reduce.7.cloned.1.call-start = ((), (), s32[]{:S(2)}) async-start(), calls=%async_computation.6 | async-start | bytes 4194304
  28.8 3.6 collective-permute-start.11
  238.3 94.3 %collective-permute-start = (bf16[128,2048]{1,0:T(8,128)(2,1)}, bf16[128,2048]{1,0:T(8,128)(2,1)}, u32[]{:S(2)}, u32[]{:S(2)}) collective-permute-start(bf16[128,2048]{1,0:T(8,128)(2,1)} %fusion.18), channel_id=1, source_target_pairs={{0,64},{64,128},{128,192},{1,65},{65,129},{129,193},{2,66},{66,130... | collective-permute-start | bytes 1572872 | tf_op jit(solution)/shard_map/ppermute | solution.py:18
  330.7 13.2 collective-permute-start.14
  338.6 16.1 collective-permute-start.1
  349.8 15.7 collective-permute-start.15
  360.7 16.0 collective-permute-start.2
  371.3 15.4 collective-permute-start.16
  382.5 14.8 collective-permute-start.3
  392.6 15.0 collective-permute-start.17
  403.3 14.2 collective-permute-start.4
  413.1 10.5 collective-permute-start.18
  419.8 10.0 collective-permute-start.5
  425.9 10.5 collective-permute-start.19
  432.1 10.5 collective-permute-start.6
  438.7 10.5 collective-permute-start.20
  451.5 10.5 collective-permute-start.21
  463.1 3.1 collective-permute-start.26
  463.8 13.8 collective-permute-start.7
  466.2 28.7 %collective-permute-start.27 = (bf16[256,2048]{1,0:T(8,128)(2,1)S(1)}, bf16[256,2048]{1,0:T(8,128)(2,1)S(1)}, u32[]{:S(2)}, u32[]{:S(2)}) collective-permute-start(bf16[256,2048]{1,0:T(8,128)(2,1)S(1)} %collective-permute-done.26), channel_id=1, source_target_pairs={{0,128},{64,192},{128,0},{192,64},{1,129},{65,193},{129,1},{193,65... | collective-permute-start | bytes 3145736 | tf_op jit(solution)/shard_map/ppermute | solution.py:12
  468.0 30.9 %collective-permute-start.24 = (bf16[2048,256]{1,0:T(8,128)(2,1)S(1)}, bf16[2048,256]{1,0:T(8,128)(2,1)}, u32[]{:S(2)}, u32[]{:S(2)}) collective-permute-start(bf16[2048,256]{1,0:T(8,128)(2,1)S(1)} %fusion.17), channel_id=1, source_target_pairs={{0,64},{64,0},{128,192},{192,128},{1,65},{65,1},{129,193},{193,129... | collective-permute-start | bytes 3145736 | tf_op jit(solution)/shard_map/ppermute | solution.py:12
  496.9 1130.1 %reduce-scatter.2.cloned.1.call-start = ((), (), s32[]{:S(2)}) async-start(), calls=%async_computation.5 | async-start | bytes 2129920 | tf_op jit(solution)/shard_map/reduce_scatter | solution.py:172
  498.9 24.2 %collective-permute-start.25 = (bf16[2048,256]{1,0:T(8,128)(2,1)}, bf16[2048,256]{1,0:T(8,128)(2,1)S(1)}, u32[]{:S(2)}, u32[]{:S(2)}) collective-permute-start(bf16[2048,256]{1,0:T(8,128)(2,1)} %collective-permute-done.24), channel_id=1, source_target_pairs={{0,128},{64,192},{128,0},{192,64},{1,129},{65,193},{129,1},{193,65... | collective-permute-start | bytes 3145736 | tf_op jit(solution)/shard_map/ppermute | solution.py:12
  529.0 3.7 collective-permute-start.23
  (60 other events, 492.8 us)
Sparse Core Ops, SparseCore 0:
  11.9 80.6 all-gather.4
  95.9 73.5 all-gather.6
  173.4 75.8 all-gather.8
  252.4 75.0 all-gather.10
  497.0 740.0 all-reduce.6
  1240.1 386.9 reduce-scatter.1
where the time goes:
time: 1640 us; the launch traced here: 1630 us
  waiting for transfers between devices  1050 us (64%)
  blocking collectives  393 us (24%)
  matrix products  63.4 us (4%)
  starting transfers between devices  51.3 us (3%)
  local copies, waits for them, and re-layouts  30.6 us (2%)
  other arithmetic  27.9 us (2%)
  between operations  17.7 us (1%)
    unnamed x7, waiting for transfers between devices  510 us
    unnamed x2, blocking collectives  393 us
    reduce_scatter x1, waiting for transfers between devices, per_device(): lax.psum_scatter(acc_down_in + passed_in, 'zero', scatter_dimension=0, ti...  388 us
    all_gather x1, waiting for transfers between devices, per_device(): lax.all_gather(mirror_in, 'zero', axis=1, tiled=True)  75.1 us
    ppermute x12, waiting for transfers between devices, partner(): lax.ppermute(value, axis, [(i, i ^ 1 << stride) for i in range(lax.axis_s...  43.7 us
    ppermute x16, starting transfers between devices, from_behind(): return lax.ppermute(block, axis, route)  40.8 us
  transfers between devices with their start and end apart: 34, of which 17 were waited for; matrix products, arithmetic and copies ran while one was open for 7% of the time, Pallas kernels for 0%

commit v1 on v0

--- a/solution.py
+++ b/solution.py
@@ -93,7 +93,9 @@
         )
     gathered = (
         lax.all_gather(proj_in, "zero", axis=1, tiled=True),
-        lax.all_gather(mirror_in, "zero", axis=1, tiled=True),
+        jnp.concatenate(
+            lax.all_to_all(jnp.stack([mirror_in] * lax.axis_size("zero")), "zero", 0, 0), axis=1
+        ),
         lax.all_gather(proj_out, "zero", axis=1, tiled=True),
         lax.all_gather(mirror_out, "zero", axis=1, tiled=True),
         lax.all_gather(norm_gain, "zero", axis=1, tiled=True),

time: 1640 us -> 1590 us (0.970)
  waiting for transfers between devices: 1050 us -> 976 us
    all_gather x1 -> x0, waiting for transfers between devices: 75.1 us -> none  [per_device(): lax.all_gather(mirror_in, 'zero', axis=1, tiled=True)]
    unnamed x7 -> x6, waiting for transfers between devices: 510 us -> 508 us
  transfers between devices with their start and end apart: 34 -> 34, of which waited for: 17 -> 11; matrix products, arithmetic and copies ran while one was open for 7% -> 7% of each run, Pallas kernels for 0% -> 0%
where the time goes in v1:
time: 1590 us; the launch traced here: 1580 us
  waiting for transfers between devices  976 us (61%)
  blocking collectives  388 us (24%)
  matrix products  74.8 us (5%)
  starting transfers between devices  63.5 us (4%)
  local copies, waits for them, and re-layouts  31.3 us (2%)
  other arithmetic  26.9 us (2%)
  between operations  17.4 us (1%)
    unnamed x6, waiting for transfers between devices  508 us
    reduce_scatter x1, waiting for transfers between devices, per_device(): lax.psum_scatter(acc_down_in + passed_in, 'zero', scatter_dimension=0, ti...  388 us
    unnamed x2, blocking collectives  388 us
    ppermute x12, waiting for transfers between devices, partner(): lax.ppermute(value, axis, [(i, i ^ 1 << stride) for i in range(lax.axis_s...  55.6 us
    ppermute x16, starting transfers between devices, from_behind(): return lax.ppermute(block, axis, route)  42.3 us
    dot_general x40, matrix products, contract(): lax.dot_general(left, right, (((left_dim,), (right_dim,)), ((), ())), pre...  37.5 us
  transfers between devices with their start and end apart: 34, of which 11 were waited for; matrix products, arithmetic and copies ran while one was open for 7% of the time, Pallas kernels for 0%

profile of v1, /device:TPU:32, one launch (start us, length us, event | category | flops | bytes accessed | tf_op | source)
XLA Modules:
  0.0 1577.7 jit_solution(17640158877081594445)
XLA Ops:
  14.7 3.5 collective-permute-done.13
  19.3 13.1 all-to-all-start
  39.9 14.2 collective-permute-done.11
  54.3 199.1 %all-reduce.4 = (bf16[2048]{0:T(1024)(128)(2,1)S(1)}, bf16[2048]{0:T(1024)(128)(2,1)S(1)}) all-reduce(bf16[2048]{0:T(1024)(128)(2,1)S(1)} %dynamic-update-slice.1, bf16[2048]{0:T(1024)(128)(2,1)S(1)} %dynamic-update-slice), channel_id=1, replica_groups=mesh['segment'=4,'zero'=64] {'zero'}, use_global_device_ids=true, to_apply=%add.1 | all-reduce | flops 4096 | bytes 16384
  253.5 3.2 copy.12
  256.7 3.5 fusion.18
  263.0 3.2 copy.13
  266.2 3.2 fusion.22
  269.3 3.6 collective-permute-start.14
  275.6 3.5 fusion.19
  285.6 3.5 fusion.23
  289.1 3.9 collective-permute-start.15
  297.7 3.5 fusion.20
  307.7 3.5 fusion.24
  311.2 3.8 collective-permute-start.16
  319.5 3.5 fusion.21
  329.6 3.5 fusion.25
  333.1 3.6 collective-permute-start.17
  351.9 3.0 fusion.171
  367.1 3.3 collective-permute-start.5
  380.2 3.6 collective-permute-start.6
  385.6 2.5 fusion.207
  391.7 7.4 collective-permute-done.20
  406.3 6.9 collective-permute-done.21
  420.0 8.8 collective-permute-done.7
  429.6 16.5 %collective-permute-done.27 = bf16[256,2048]{1,0:T(8,128)(2,1)S(1)} collective-permute-done((bf16[256,2048]{1,0:T(8,128)(2,1)S(1)}, bf16[256,2048]{1,0:T(8,128)(2,1)S(1)}, u32[]{:S(2)}, u32[]{:S(2)}) %collective-permute-start.27) | collective-permute-done | bytes 1048608 | tf_op jit(solution)/shard_map/ppermute | solution.py:12
  450.2 2.6 collective-permute-start.25
  456.8 18.5 %collective-permute-done.25 = bf16[2048,256]{1,0:T(8,128)(2,1)S(1)} collective-permute-done((bf16[2048,256]{1,0:T(8,128)(2,1)}, bf16[2048,256]{1,0:T(8,128)(2,1)S(1)}, u32[]{:S(2)}, u32[]{:S(2)}) %collective-permute-start.25) | collective-permute-done | bytes 1048608 | tf_op jit(solution)/shard_map/ppermute | solution.py:12
  482.0 2.8 collective-permute-done.23
  484.9 188.7 %all-reduce.2 = f32[2048]{0:T(1024)S(1)} all-reduce(f32[2048]{0:T(1024)S(1)} %convert_add_fusion.2), channel_id=2, replica_groups=mesh['segment'=4,'zero'=64] {'zero'}, use_global_device_ids=true, to_apply=%region_62.63.clone | all-reduce | flops 2048 | bytes 16384
  674.2 507.2 %all-reduce.7.cloned.1.call-done = f32[256,2048]{1,0:T(8,128)} async-done(((f32[256,2048]{1,0:T(8,128)}), f32[256,2048]{1,0:T(8,128)}) %all-reduce.7.cloned.1.call-update) | async-done | bytes 2097168
  1182.9 388.1 %reduce-scatter.2.cloned.1.call-done = f32[32,256]{1,0:T(8,128)} async-done(((f32[2048,256]{1,0:T(8,128)}), f32[32,256]{1,0:T(8,128)}) %reduce-scatter.2.cloned.1.call-update) | async-done | bytes 32784 | tf_op jit(solution)/shard_map/reduce_scatter | solution.py:174
  (335 shorter events, 121.4 us)
Async XLA Ops:
  7.2 246.3 %all-gather.4.cloned.1.call-start = ((), (), s32[]{:S(2)}) async-start(), calls=%async_computation.2 | async-start | bytes 2129920 | tf_op jit(solution)/shard_map/all_gather | solution.py:99
  8.6 248.1 %all-gather.6.cloned.1.call-start = ((), (), s32[]{:S(2)}) async-start(), calls=%async_computation.3 | async-start | bytes 1064960 | tf_op jit(solution)/shard_map/all_gather | solution.py:95
  9.3 3.2 collective-permute-start.8
  9.4 5.0 collective-permute-start.12
  9.9 28.7 %collective-permute-start.10 = (bf16[1,32]{1,0:T(2,128)(2,1)}, bf16[1,32]{1,0:T(2,128)(2,1)S(1)}, u32[]{:S(2)}, u32[]{:S(2)}) collective-permute-start(bf16[1,32]{1,0:T(2,128)(2,1)} %param.7), channel_id=1, source_target_pairs={{0,64},{64,0},{128,192},{192,128},{1,65},{65,1},{129,193},{193,129... | collective-permute-start | bytes 200 | tf_op jit(solution)/shard_map/ppermute | solution.py:12
  12.5 19.9 %collective-permute-start.9 = (bf16[1,4,2048]{2,0,1:T(2,128)(2,1)S(1)}, bf16[1,4,2048]{2,0,1:T(2,128)(2,1)S(1)}, u32[]{:S(2)}, u32[]{:S(2)}) collective-permute-start(bf16[1,4,2048]{2,0,1:T(2,128)(2,1)S(1)} %collective-permute-done.8), channel_id=1, source_target_pairs={{0,128},{64,192},{128,0},{192,64},{1,129},{65,193},{129,1},{193,65... | collective-permute-start | bytes 49160 | tf_op jit(solution)/shard_map/ppermute | solution.py:12
  14.4 3.7 collective-permute-start.13
  19.3 246.9 %all-to-all-start = ((bf16[64,1,32,256]{3,2,1,0:T(8,128)(2,1)}), bf16[64,1,32,256]{3,2,1,0:T(8,128)(2,1)}, u32[]{:S(2)}, u32[]{:S(2)}) async-start(bf16[64,1,32,256]{3,2,1,0:T(8,128)(2,1)} %stack.2), calls=%async_computation | async-start | bytes 2097152 | tf_op jit(solution)/shard_map/all_to_all | solution.py:97
  32.4 230.6 %all-gather.8.cloned.1.call-start = ((), (), s32[]{:S(2)}) async-start(), calls=%async_computation.4 | async-start | bytes 2129920 | tf_op jit(solution)/shard_map/all_gather | solution.py:100
  33.2 1148.3 %all-reduce.7.cloned.1.call-start = ((), (), s32[]{:S(2)}) async-start(), calls=%async_computation.6 | async-start | bytes 4194304
  38.7 15.4 collective-permute-start.11
  260.2 12.8 collective-permute-start
  269.3 13.9 collective-permute-start.14
  279.1 16.2 %collective-permute-start.1 = (bf16[128,2048]{1,0:T(8,128)(2,1)}, bf16[128,2048]{1,0:T(8,128)(2,1)}, u32[]{:S(2)}, u32[]{:S(2)}) collective-permute-start(bf16[128,2048]{1,0:T(8,128)(2,1)} %fusion.19), channel_id=1, source_target_pairs={{0,64},{64,128},{128,192},{1,65},{65,129},{129,193},{2,66},{66,130... | collective-permute-start | bytes 1572872 | tf_op jit(solution)/shard_map/ppermute | solution.py:18
  289.1 16.2 %collective-permute-start.15 = (bf16[128,2048]{1,0:T(8,128)(2,1)}, bf16[128,2048]{1,0:T(8,128)(2,1)}, u32[]{:S(2)}, u32[]{:S(2)}) collective-permute-start(bf16[128,2048]{1,0:T(8,128)(2,1)} %fusion.23), channel_id=1, source_target_pairs={{64,0},{128,64},{192,128},{65,1},{129,65},{193,129},{66,2},{130,66... | collective-permute-start | bytes 1572872 | tf_op jit(solution)/shard_map/ppermute | solution.py:18
  301.2 16.0 %collective-permute-start.2 = (bf16[128,2048]{1,0:T(8,128)(2,1)}, bf16[128,2048]{1,0:T(8,128)(2,1)}, u32[]{:S(2)}, u32[]{:S(2)}) collective-permute-start(bf16[128,2048]{1,0:T(8,128)(2,1)} %fusion.20), channel_id=1, source_target_pairs={{0,64},{64,128},{128,192},{1,65},{65,129},{129,193},{2,66},{66,130... | collective-permute-start | bytes 1572872 | tf_op jit(solution)/shard_map/ppermute | solution.py:18
  311.2 16.0 %collective-permute-start.16 = (bf16[128,2048]{1,0:T(8,128)(2,1)}, bf16[128,2048]{1,0:T(8,128)(2,1)}, u32[]{:S(2)}, u32[]{:S(2)}) collective-permute-start(bf16[128,2048]{1,0:T(8,128)(2,1)} %fusion.24), channel_id=1, source_target_pairs={{64,0},{128,64},{192,128},{65,1},{129,65},{193,129},{66,2},{130,66... | collective-permute-start | bytes 1572872 | tf_op jit(solution)/shard_map/ppermute | solution.py:18
  323.0 14.9 collective-permute-start.3
  333.1 15.1 collective-permute-start.17
  343.8 20.9 %collective-permute-start.4 = (bf16[128,2048]{1,0:T(8,128)(2,1)S(1)}, bf16[128,2048]{1,0:T(8,128)(2,1)S(1)}, u32[]{:S(2)}, u32[]{:S(2)}) collective-permute-start(bf16[128,2048]{1,0:T(8,128)(2,1)S(1)} %fusion.92), channel_id=1, source_target_pairs={{64,0},{128,64},{192,128},{65,1},{129,65},{193,129},{66,2},{130,66... | collective-permute-start | bytes 1572872 | tf_op jit(solution)/shard_map/ppermute | solution.py:18
  355.6 15.3 collective-permute-start.18
  367.1 10.8 collective-permute-start.5
  374.5 10.5 collective-permute-start.19
  380.2 10.9 collective-permute-start.6
  388.6 10.5 collective-permute-start.20
  402.7 10.5 collective-permute-start.21
  415.0 13.8 collective-permute-start.7
  417.4 28.7 %collective-permute-start.27 = (bf16[256,2048]{1,0:T(8,128)(2,1)S(1)}, bf16[256,2048]{1,0:T(8,128)(2,1)S(1)}, u32[]{:S(2)}, u32[]{:S(2)}) collective-permute-start(bf16[256,2048]{1,0:T(8,128)(2,1)S(1)} %collective-permute-done.26), channel_id=1, source_target_pairs={{0,128},{64,192},{128,0},{192,64},{1,129},{65,193},{129,1},{193,65... | collective-permute-start | bytes 3145736 | tf_op jit(solution)/shard_map/ppermute | solution.py:12
  419.2 30.9 %collective-permute-start.24 = (bf16[2048,256]{1,0:T(8,128)(2,1)S(1)}, bf16[2048,256]{1,0:T(8,128)(2,1)}, u32[]{:S(2)}, u32[]{:S(2)}) collective-permute-start(bf16[2048,256]{1,0:T(8,128)(2,1)S(1)} %fusion.17), channel_id=1, source_target_pairs={{0,64},{64,0},{128,192},{192,128},{1,65},{65,1},{129,193},{193,129... | collective-permute-start | bytes 3145736 | tf_op jit(solution)/shard_map/ppermute | solution.py:12
  448.1 1122.9 %reduce-scatter.2.cloned.1.call-start = ((), (), s32[]{:S(2)}) async-start(), calls=%async_computation.5 | async-start | bytes 2129920 | tf_op jit(solution)/shard_map/reduce_scatter | solution.py:174
  450.2 25.1 %collective-permute-start.25 = (bf16[2048,256]{1,0:T(8,128)(2,1)}, bf16[2048,256]{1,0:T(8,128)(2,1)S(1)}, u32[]{:S(2)}, u32[]{:S(2)}) collective-permute-start(bf16[2048,256]{1,0:T(8,128)(2,1)} %collective-permute-done.24), channel_id=1, source_target_pairs={{0,128},{64,192},{128,0},{192,64},{1,129},{65,193},{129,1},{193,65... | collective-permute-start | bytes 3145736 | tf_op jit(solution)/shard_map/ppermute | solution.py:12
  481.2 3.7 collective-permute-start.23
  (59 other events, 592.1 us)
Sparse Core Ops, SparseCore 0:
  11.9 85.4 all-gather.3
  100.7 73.6 all-gather.5
  178.2 76.2 all-gather.7
  448.2 733.1 all-reduce.6
  1184.4 386.6 reduce-scatter.1
